TPU v7x, 32 devices: a whole 2x2x4 slice. The times are simulated.
32 devices in a mesh: groups: 2 (over x), inst: 8 (over z, y), tp: 2 (over core).
Axes of the slice: x: 2, y: 2, z: 4, core: 2. Of those that a mesh axis runs over, the one named last changes fastest.
Arguments:
- queries: bfloat16 [4, 512, 3072], P(None, ('groups', 'inst'), 'tp'), parts along dimension 1, may hold values from -130 to 130
- new_kv: bfloat16 [4, 512, 256], P(None, ('groups', 'inst')), parts along dimension 1, may hold values from -4.5 to 4.5
- cache_pool: bfloat16 [98304, 256], P(('groups', 'inst')), parts along dimension 0, may hold values from -6 to 6
- lengths: int32 [16, 32], P('groups'), parts along dimension 0, may hold values from 1 to 2, as said below
- anchor: int32 [16, 32], P('groups'), parts along dimension 0, may hold values from 0 to 7, as said below
- out_weight: bfloat16 [3072, 3072], P('tp'), may hold values from -0.875 to 0.875
Outputs:
- attended: bfloat16 [4, 512, 3072], P(None, ('groups', 'inst'), 'tp'), parts along dimension 1
There are 2 independent parts, one for each index of `groups`. A program takes and returns all parts, laid end to end along the dimension named above; an argument that names none is the same for every part. Nothing has to cross between parts.
Inputs may be any that keep to these rules, and one draw needn't show every extreme that they name: `lengths`: in every instance exactly 16 requests hold 2 blocks and the others one; the requests' blocks lie in the instance's pool in slot order, each right after the one before, filling its 48 blocks. anchor[d, j] is the instance whose request in slot j moves to slot j of instance d, or d where the slot stays. Exactly 7 slots move; for each of them the source is the destination rotated by one amount, nonzero and different for each moving slot, and one of these amounts is half the number of instances, rounded down; so every instance sends and receives exactly 7 requests, at most one to or from any other instance.
All inputs are finite; a program needn't handle non-finite values.
Results may differ from a plain program's by a relative error of at most 0.009.
Values may be sent and summed in bfloat16 or wider, within the bound.
A program may use at most 128 MiB of HBM per device.

v0:
```python
import functools
import math

import jax
import jax.numpy as jnp
from jax import lax
from jax.experimental import pallas as pl
from jax.experimental.pallas import tpu as pltpu
from jax.sharding import PartitionSpec as P

HDIM = 128
BLK = 128
MAXB = 2
MESH = pl.DeviceIdType.MESH
NT = (((1,), (1,)), ((), ()))


def grouped(count, unroll, fn):
    full = count // unroll
    if full == 1:
        fn([i for i in range(unroll)])
    elif full > 1:

        def step(g, carry):
            fn([g * unroll + u for u in range(unroll)])
            return carry

        lax.fori_loop(0, full, step, 0)
    rest = list(range(full * unroll, count))
    if rest:
        fn(rest)


def kernel(
    n, cols, q_hbm, kv_hbm, pool_hbm, len_hbm, anc_hbm, w_hbm, out_ref,
    q_in, kv_in, pool, w_buf, item, res, fin, lhs, causal,
    q_out, q_got, r_out, r_got, o_out, o_got, m_out, m_got, main, back, moved_lhs, spread,
    len_s, anc_s, shift_s, off_s, stay_s, nxt_s, slot_s, used_s, free_s, pos_s,
    in_sem, w_sem, q_send, q_recv, r_send, r_recv, o_send, o_recv, m_send, m_recv,
):
    steps, slots, width = q_in.shape
    heads = width // HDIM
    rows = steps * heads
    span = rows + 2 * steps
    window = MAXB * BLK
    blocks = pool_hbm.shape[0]
    half = out_ref.shape[2]
    chunks = half // cols
    peers = n - 1
    stays = slots - peers
    me = lax.axis_index("inst")
    tp = lax.axis_index("tp")

    copy_q = pltpu.make_async_copy(q_hbm, q_in, in_sem.at[0])
    copy_kv = pltpu.make_async_copy(kv_hbm, kv_in, in_sem.at[1])
    copy_pool = pltpu.make_async_copy(pool_hbm, pool.at[pl.ds(0, blocks)], in_sem.at[2])
    copy_len = pltpu.make_async_copy(len_hbm, len_s, in_sem.at[3])
    copy_anc = pltpu.make_async_copy(anc_hbm, anc_s, in_sem.at[4])
    copy_len.start()
    copy_anc.start()
    copy_q.start()
    copy_kv.start()
    copy_w = []
    for c in range(2 * chunks):
        side = (1 - tp) if c < chunks else tp
        column = pl.multiple_of(side * half + (c % chunks) * cols, cols)
        copy_w.append(
            pltpu.make_async_copy(w_hbm.at[:, pl.ds(column, cols)], w_buf.at[c], w_sem.at[c])
        )

    def peer(k):
        return {"inst": lax.rem(me + k, n)}

    barrier = pltpu.get_barrier_semaphore()
    for k in range(1, n):
        pl.semaphore_signal(barrier, inc=1, device_id=peer(k), device_id_type=MESH)
    pl.semaphore_signal(barrier, inc=1, device_id={"tp": 1 - tp}, device_id_type=MESH)

    def scan_slot(j, carry):
        off, found = carry
        turn = me - anc_s[me, j]
        turn = jnp.where(turn < 0, turn + n, turn)
        shift_s[j] = turn
        off_s[j] = off
        found = tuple(jnp.where(turn == k + 1, j, found[k]) for k in range(peers))
        return off + len_s[me, j], found

    copy_len.wait()
    copy_anc.wait()
    _, found = lax.fori_loop(
        0, slots, scan_slot, (jnp.int32(0), tuple(jnp.int32(-1) for _ in range(peers))),
        unroll=8,
    )

    flat = item.reshape(slots * span, HDIM)
    copy_q.wait()
    copy_kv.wait()
    copy_pool.start()
    for copy in copy_w:
        copy.start()
    for t in range(steps):
        for h in range(heads):
            flat[pl.ds(t * heads + h, slots, stride=span), :] = q_in[
                t, :, h * HDIM : (h + 1) * HDIM
            ].astype(jnp.float32)
        for part in range(2):
            flat[pl.ds(rows + part * steps + t, slots, stride=span), :] = kv_in[
                t, :, part * HDIM : (part + 1) * HDIM
            ].astype(jnp.float32)

    def item_of(slot):
        return item[slot]

    for k in range(peers):
        q_out[k] = item_of(jnp.maximum(found[k], 0)).astype(jnp.bfloat16)
    pl.semaphore_wait(barrier, n)

    def send_q(k):
        return pltpu.make_async_remote_copy(
            src_ref=q_out.at[k], dst_ref=q_got.at[k], send_sem=q_send.at[k],
            recv_sem=q_recv.at[k], device_id=peer(n - 1 - k), device_id_type=MESH,
        )

    def send_r(k):
        return pltpu.make_async_remote_copy(
            src_ref=r_out.at[k], dst_ref=r_got.at[k], send_sem=r_send.at[k],
            recv_sem=r_recv.at[k], device_id=peer(k + 1), device_id_type=MESH,
        )

    def send_o(c):
        return pltpu.make_async_remote_copy(
            src_ref=o_out.at[c], dst_ref=o_got.at[c], send_sem=o_send.at[c],
            recv_sem=o_recv.at[c], device_id={"tp": 1 - tp}, device_id_type=MESH,
        )

    def send_m(c):
        return pltpu.make_async_remote_copy(
            src_ref=m_out.at[c], dst_ref=m_got.at[c], send_sem=m_send.at[c],
            recv_sem=m_recv.at[c], device_id={"tp": 1 - tp}, device_id_type=MESH,
        )

    for k in range(peers):
        send_q(k).start()

    def scan_next(i, cur):
        j = slots - 1 - i
        cur = jnp.where(shift_s[j] == 0, j, cur)
        nxt_s[j] = cur
        return cur

    lax.fori_loop(0, slots, scan_next, jnp.int32(slots - 1), unroll=True)

    def scan_stay(i, cur):
        stay_s[i] = cur
        return nxt_s[jnp.minimum(cur + 1, slots - 1)]

    lax.fori_loop(0, slots, scan_stay, nxt_s[0], unroll=True)
    spare = jnp.int32(0)
    for k in range(peers):
        slot_s[k] = jnp.where(found[k] >= 0, found[k], stay_s[stays + spare])
        used_s[k] = jnp.where(found[k] >= 0, 1, 0)
        spare = spare + jnp.where(found[k] >= 0, 0, 1)
    nxt = jnp.int32(peers - 1)
    for k in reversed(range(peers)):
        nxt = jnp.where(found[k] >= 0, nxt, k)
        nxt_s[k] = nxt
    nxt = nxt_s[0]
    for k in range(peers):
        free_s[k] = nxt
        nxt = nxt_s[jnp.minimum(nxt + 1, peers - 1)]

    def scan_pos(j, count):
        turn = shift_s[j]
        extra = free_s[jnp.clip(count - stays, 0, peers - 1)]
        rest = jnp.where(count < stays, count, stays + extra)
        pos_s[j] = jnp.where(turn > 0, stays + turn - 1, rest)
        return count + jnp.where(turn > 0, 0, 1)

    lax.fori_loop(0, slots, scan_pos, jnp.int32(0), unroll=True)

    pool[blocks] = jnp.zeros((BLK, 2 * HDIM), pool.dtype)
    row_id = lax.broadcasted_iota(jnp.int32, (rows, 2 * steps), 0)
    col_id = lax.broadcasted_iota(jnp.int32, (rows, 2 * steps), 1)
    causal[...] = jnp.where((col_id < steps) & (row_id >= col_id * heads), 0.0, -jnp.inf)
    copy_pool.wait()

    factor = math.log2(math.e) / math.sqrt(HDIM)
    key_id = lax.broadcasted_iota(jnp.int32, (1, window), 1)

    def cached(start):
        return jnp.concatenate([pool[start + b] for b in range(MAXB)], axis=0)

    def attend(items, owners):
        added = [x[rows:] for x in items]
        new_keys = [x.astype(jnp.bfloat16) for x in added]
        new_values = [pltpu.roll(x, steps, 0).astype(jnp.bfloat16) for x in added]
        items = [x[:rows].astype(jnp.bfloat16) for x in items]
        starts = [off_s[j] for j in owners]
        scores, fresh = [], []
        for x, y, j, start in zip(items, new_keys, owners, starts):
            s = lax.dot_general(
                x, cached(start)[:, :HDIM], NT, preferred_element_type=jnp.float32
            )
            scores.append(jnp.where(key_id < len_s[me, j] * BLK, s, -jnp.inf))
            s = lax.dot_general(x, y, NT, preferred_element_type=jnp.float32)
            fresh.append(s + causal[...])
        tops = [
            jnp.maximum(jnp.max(s, axis=1, keepdims=True), jnp.max(f, axis=1, keepdims=True))
            for s, f in zip(scores, fresh)
        ]
        scores = [jnp.exp2((s - m) * factor) for s, m in zip(scores, tops)]
        fresh = [jnp.exp2((f - m) * factor) for f, m in zip(fresh, tops)]
        results = []
        for y, s, f, start in zip(new_values, scores, fresh, starts):
            total = jnp.sum(s, axis=1, keepdims=True) + jnp.sum(f, axis=1, keepdims=True)
            o = jnp.dot(
                s.astype(jnp.bfloat16), cached(start)[:, HDIM:],
                preferred_element_type=jnp.float32,
            )
            o = o + jnp.dot(
                f.astype(jnp.bfloat16), y, preferred_element_type=jnp.float32
            )
            results.append(o / total)
        return results

    def put(i, value):
        res[i] = value

    def stay_group(base):
        def run(indices):
            owners = [stay_s[base + i] for i in indices]
            for i, o in zip(indices, attend([item_of(j) for j in owners], owners)):
                put(base + i, o)

        return run

    def move_group(ks):
        owners = [slot_s[k] for k in ks]
        for k in ks:
            send_q(k).wait_recv()
        items = [
            jnp.where(used_s[k] > 0, q_got[k].astype(jnp.float32), item_of(j))
            for k, j in zip(ks, owners)
        ]
        for k, o in zip(ks, attend(items, owners)):
            put(stays + k, o)
            r_out[k] = o.astype(jnp.bfloat16)
        for k in ks:
            send_r(k).start()

    early = stays // 2 // 5 * 5
    grouped(early, 5, stay_group(0))
    grouped(peers, 7, move_group)
    grouped(stays - early, 5, stay_group(early))

    def gather(j, carry):
        own = res[pos_s[j]]
        fin[pl.ds(pl.multiple_of(j * rows, 8), rows), :] = jnp.where(
            shift_s[j] > 0, jnp.zeros_like(own), own
        )
        return carry

    lax.fori_loop(0, slots, gather, 0, unroll=8)
    for t in range(steps):
        for h in range(heads):
            lhs[t * slots : (t + 1) * slots, h * HDIM : (h + 1) * HDIM] = fin[
                pl.ds(t * heads + h, slots, stride=rows), :
            ].astype(jnp.bfloat16)
    for c in range(chunks):
        copy_w[c].wait()
        o_out[c] = jnp.dot(lhs[...], w_buf[c], preferred_element_type=jnp.float32).astype(
            jnp.bfloat16
        )
        send_o(c).start()
    for c in range(chunks):
        copy_w[chunks + c].wait()
        main[c] = jnp.dot(lhs[...], w_buf[chunks + c], preferred_element_type=jnp.float32)

    pad = back.shape[0]
    row_id = lax.broadcasted_iota(jnp.int32, (slots, steps * pad), 0)
    col_id = lax.broadcasted_iota(jnp.int32, (slots, steps * pad), 1)
    turns = jnp.zeros((slots, steps * pad), jnp.int32)
    for j in range(slots):
        turns = jnp.where(row_id == j, shift_s[j], turns)
    for t in range(steps):
        spread[t * slots : (t + 1) * slots, :] = jnp.where(
            (turns > 0) & (col_id == turns + (t * pad - 1)), 1.0, 0.0
        ).astype(jnp.bfloat16)

    for k in range(peers, pad):
        back[k] = jnp.zeros((rows, HDIM), jnp.float32)
    for k in range(peers):
        send_r(k).wait_recv()
        back[k] = r_got[k].astype(jnp.float32)
    flat_back = back.reshape(pad * rows, HDIM)
    for t in range(steps):
        for h in range(heads):
            moved_lhs[t * pad : (t + 1) * pad, h * HDIM : (h + 1) * HDIM] = flat_back[
                pl.ds(t * heads + h, pad, stride=rows), :
            ]
    moved = moved_lhs[...].astype(jnp.bfloat16)
    for c in range(chunks):
        m_out[c] = jnp.dot(moved, w_buf[c], preferred_element_type=jnp.float32).astype(
            jnp.bfloat16
        )
        send_m(c).start()
    for c in range(chunks):
        own = jnp.dot(moved, w_buf[chunks + c], preferred_element_type=jnp.float32)
        send_o(c).wait_recv()
        send_m(c).wait_recv()
        own = (own + m_got[c].astype(jnp.float32)).astype(jnp.bfloat16)
        own = jnp.dot(spread[...], own, preferred_element_type=jnp.float32)
        own = (own + (main[c] + o_got[c].astype(jnp.float32))).astype(out_ref.dtype)
        for t in range(steps):
            out_ref[t, :, c * cols : (c + 1) * cols] = own[t * slots : (t + 1) * slots]
    for k in range(peers):
        send_q(k).wait_send()
        send_r(k).wait_send()
    for c in range(chunks):
        send_o(c).wait_send()
        send_m(c).wait_send()


def body(n, queries, new_kv, cache_pool, lengths, anchor, out_weight):
    steps, slots, width = queries.shape
    features = out_weight.shape[1]
    half = features // lax.axis_size("tp")
    cols = 768 if half % 768 == 0 else half
    chunks = half // cols
    rows = steps * (width // HDIM)
    span = rows + 2 * steps
    peers = n - 1
    pad = -(-peers // 8) * 8
    blocks = cache_pool.shape[0] // BLK
    bf16, f32, i32 = jnp.bfloat16, jnp.float32, jnp.int32
    dma = pltpu.SemaphoreType.DMA
    anywhere = pl.BlockSpec(memory_space=pltpu.HBM)
    cache = cache_pool.reshape(blocks, BLK, 2 * HDIM)
    queries, new_kv, cache, lengths, anchor, out_weight = (
        pltpu.with_memory_space_constraint(x, pltpu.HBM)
        for x in (queries, new_kv, cache, lengths, anchor, out_weight)
    )
    return pl.pallas_call(
        functools.partial(kernel, n, cols),
        out_shape=jax.ShapeDtypeStruct((steps, slots, half), bf16),
        in_specs=[anywhere] * 6,
        out_specs=pl.BlockSpec(memory_space=pltpu.VMEM),
        scratch_shapes=[
            pltpu.VMEM(queries.shape, bf16),
            pltpu.VMEM(new_kv.shape, bf16),
            pltpu.VMEM((blocks + MAXB - 1, BLK, 2 * HDIM), bf16),
            pltpu.VMEM((2 * chunks, width, cols), bf16),
            pltpu.VMEM((slots, span, HDIM), f32),
            pltpu.VMEM((slots, rows, HDIM), f32),
            pltpu.VMEM((slots * rows, HDIM), f32),
            pltpu.VMEM((steps * slots, width), bf16),
            pltpu.VMEM((rows, 2 * steps), f32),
            pltpu.VMEM((peers, span, HDIM), bf16),
            pltpu.VMEM((peers, span, HDIM), bf16),
            pltpu.VMEM((peers, rows, HDIM), bf16),
            pltpu.VMEM((peers, rows, HDIM), bf16),
            pltpu.VMEM((chunks, steps * slots, cols), bf16),
            pltpu.VMEM((chunks, steps * slots, cols), bf16),
            pltpu.VMEM((chunks, steps * pad, cols), bf16),
            pltpu.VMEM((chunks, steps * pad, cols), bf16),
            pltpu.VMEM((chunks, steps * slots, cols), f32),
            pltpu.VMEM((pad, rows, HDIM), f32),
            pltpu.VMEM((steps * pad, width), f32),
            pltpu.VMEM((steps * slots, steps * pad), bf16),
        ]
        + [pltpu.SMEM(lengths.shape, i32), pltpu.SMEM(anchor.shape, i32)]
        + [pltpu.SMEM((max(slots, n),), i32)] * 8
        + [dma((5,)), dma((2 * chunks,))]
        + [dma((peers,))] * 4
        + [dma((chunks,))] * 4,
        compiler_params=pltpu.CompilerParams(
            collective_id=0, has_side_effects=True, vmem_limit_bytes=48 * 1024 * 1024
        ),
    )(queries, new_kv, cache, lengths, anchor, out_weight)


def solution(mesh):
    n = mesh.shape["inst"]
    placed = (
        P(None, ("groups", "inst"), "tp"),
        P(None, ("groups", "inst"), None),
        P(("groups", "inst"), None),
        P("groups", None),
        P("groups", None),
        P("tp", None),
    )
    return jax.shard_map(
        functools.partial(body, n),
        mesh=mesh,
        in_specs=placed,
        out_specs=P(None, ("groups", "inst"), "tp"),
        check_vma=False,
    )
```

profile of v0, /device:TPU:0, one launch (start us, length us, event | category | flops | bytes accessed | tf_op | source)
XLA Modules:
  0.0 18.8 jit_solution(8744175839718039740)
XLA Ops:
  0.0 18.0 %shard_map.64 = bf16[4,32,1536]{2,1,0:T(8,128)(2,1)S(1)} custom-call(bf16[4,32,1536]{2,1,0:T(8,128)(2,1)} %q_hbm.1, bf16[4,32,256]{2,1,0:T(8,128)(2,1)} %kv_hbm.1, bf16[48,128,256]{2,1,0:T(8,128)(2,1)} %bitcast.1, s32[8,32]{1,0:T(8,128)} %len_hbm.1, s32[8,32]{1,0:T(8,128)} %anc_hbm.1, bf16[1536,3072]{1,0:T(8,128)(2,1)} %w_hbm.1), custom_call_target="tpu_custom_call" | custom-call | tf_op jit(solution)/shard_map/pallas_call | solution.py:343
  18.1 0.7 %copy.8 = bf16[4,32,1536]{2,1,0:T(8,128)(2,1)} copy(bf16[4,32,1536]{2,1,0:T(8,128)(2,1)S(1)} %shard_map.64) | data formatting | bytes 786432
where the time goes:
time: 19 us; the launch traced here: 18.8 us
  Pallas kernels  18 us (95%)
  local copies, waits for them, and re-layouts  0.75 us (4%)
    pallas_call x1, Pallas kernels, body(): pl.pallas_call(functools.partial(kernel, n, cols), out_shape=jax.ShapeDty...  18 us
    unnamed x1, local copies, waits for them, and re-layouts  0.75 us

commit v1 on v0

--- a/solution.py
+++ b/solution.py
@@ -12,6 +12,8 @@
 BLK = 128
 MAXB = 2
 MESH = pl.DeviceIdType.MESH
+EDGE = 1
+MAIN_FIRST = 2
 NT = (((1,), (1,)), ((), ()))
 
 
@@ -32,11 +34,12 @@
 
 
 def kernel(
-    n, cols, q_hbm, kv_hbm, pool_hbm, len_hbm, anc_hbm, w_hbm, out_ref,
+    n, edge, cols, q_hbm, kv_hbm, pool_hbm, len_hbm, anc_hbm, w_hbm, out_ref,
     q_in, kv_in, pool, w_buf, item, res, fin, lhs, causal,
-    q_out, q_got, r_out, r_got, o_out, o_got, m_out, m_got, main, back, moved_lhs, spread,
+    q_out, q_got, r_out, r_got, o_out, o_got, m_out, m_got, main, own, back, moved_lhs, spread,
+    push_out, push_got,
     len_s, anc_s, shift_s, off_s, stay_s, nxt_s, slot_s, used_s, free_s, pos_s,
-    in_sem, w_sem, q_send, q_recv, r_send, r_recv, o_send, o_recv, m_send, m_recv,
+    in_sem, w_sem, q_send, q_recv, r_send, r_recv, x_send, o_recv, m_recv, p_sem,
 ):
     steps, slots, width = q_in.shape
     heads = width // HDIM
@@ -50,16 +53,22 @@
     stays = slots - peers
     me = lax.axis_index("inst")
     tp = lax.axis_index("tp")
-
-    copy_q = pltpu.make_async_copy(q_hbm, q_in, in_sem.at[0])
-    copy_kv = pltpu.make_async_copy(kv_hbm, kv_in, in_sem.at[1])
-    copy_pool = pltpu.make_async_copy(pool_hbm, pool.at[pl.ds(0, blocks)], in_sem.at[2])
-    copy_len = pltpu.make_async_copy(len_hbm, len_s, in_sem.at[3])
-    copy_anc = pltpu.make_async_copy(anc_hbm, anc_s, in_sem.at[4])
+    crowded = peers <= slots // 4
+    mirror = n - 1 - me
+    is_early = me < edge
+    is_late = mirror < edge
+    push_k = 2 * jnp.minimum(me, mirror)
+
+    copy_len = pltpu.make_async_copy(len_hbm, len_s, in_sem.at[0])
+    copy_anc = pltpu.make_async_copy(anc_hbm, anc_s, in_sem.at[1])
+    copy_q = pltpu.make_async_copy(q_hbm, q_in, in_sem.at[2])
+    copy_kv = pltpu.make_async_copy(kv_hbm, kv_in, in_sem.at[3])
+    copy_pool = pltpu.make_async_copy(pool_hbm, pool.at[pl.ds(0, blocks)], in_sem.at[4])
     copy_len.start()
     copy_anc.start()
     copy_q.start()
     copy_kv.start()
+    copy_pool.start()
     copy_w = []
     for c in range(2 * chunks):
         side = (1 - tp) if c < chunks else tp
@@ -72,8 +81,12 @@
         return {"inst": lax.rem(me + k, n)}
 
     barrier = pltpu.get_barrier_semaphore()
-    for k in range(1, n):
-        pl.semaphore_signal(barrier, inc=1, device_id=peer(k), device_id_type=MESH)
+    for k in range(peers):
+
+        @pl.when(jnp.logical_not(is_late & (push_k == k)))
+        def _():
+            pl.semaphore_signal(barrier, inc=1, device_id=peer(k + 1), device_id_type=MESH)
+
     pl.semaphore_signal(barrier, inc=1, device_id={"tp": 1 - tp}, device_id_type=MESH)
 
     def scan_slot(j, carry):
@@ -95,9 +108,6 @@
     flat = item.reshape(slots * span, HDIM)
     copy_q.wait()
     copy_kv.wait()
-    copy_pool.start()
-    for copy in copy_w:
-        copy.start()
     for t in range(steps):
         for h in range(heads):
             flat[pl.ds(t * heads + h, slots, stride=span), :] = q_in[
@@ -113,34 +123,67 @@
 
     for k in range(peers):
         q_out[k] = item_of(jnp.maximum(found[k], 0)).astype(jnp.bfloat16)
-    pl.semaphore_wait(barrier, n)
 
     def send_q(k):
         return pltpu.make_async_remote_copy(
-            src_ref=q_out.at[k], dst_ref=q_got.at[k], send_sem=q_send.at[k],
-            recv_sem=q_recv.at[k], device_id=peer(n - 1 - k), device_id_type=MESH,
+            src_ref=q_out.at[k], dst_ref=q_got.at[k], send_sem=q_send,
+            recv_sem=q_recv, device_id=peer(n - 1 - k), device_id_type=MESH,
         )
 
     def send_r(k):
         return pltpu.make_async_remote_copy(
-            src_ref=r_out.at[k], dst_ref=r_got.at[k], send_sem=r_send.at[k],
-            recv_sem=r_recv.at[k], device_id=peer(k + 1), device_id_type=MESH,
+            src_ref=r_out.at[k], dst_ref=r_got.at[k], send_sem=r_send,
+            recv_sem=r_recv, device_id=peer(k + 1), device_id_type=MESH,
         )
 
     def send_o(c):
         return pltpu.make_async_remote_copy(
-            src_ref=o_out.at[c], dst_ref=o_got.at[c], send_sem=o_send.at[c],
-            recv_sem=o_recv.at[c], device_id={"tp": 1 - tp}, device_id_type=MESH,
+            src_ref=o_out.at[c], dst_ref=o_got.at[c], send_sem=x_send.at[0],
+            recv_sem=o_recv, device_id={"tp": 1 - tp}, device_id_type=MESH,
         )
 
     def send_m(c):
         return pltpu.make_async_remote_copy(
-            src_ref=m_out.at[c], dst_ref=m_got.at[c], send_sem=m_send.at[c],
+            src_ref=m_out.at[c], dst_ref=m_got.at[c], send_sem=x_send.at[1],
             recv_sem=m_recv.at[c], device_id={"tp": 1 - tp}, device_id_type=MESH,
         )
 
+    push = pltpu.make_async_remote_copy(
+        src_ref=push_out, dst_ref=push_got.at[tp], send_sem=p_sem.at[0],
+        recv_sem=p_sem.at[1], device_id={"inst": mirror}, device_id_type=MESH,
+    )
+    relay = pltpu.make_async_remote_copy(
+        src_ref=push_got.at[tp], dst_ref=push_got.at[tp], send_sem=p_sem.at[0],
+        recv_sem=p_sem.at[2], device_id={"tp": 1 - tp}, device_id_type=MESH,
+    )
+
+    group = 5
+    full = stays // group
+
+    def all_but_one(fewer, ref, sem):
+        @pl.when(fewer)
+        def _():
+            if peers > 1:
+                part = ref.at[pl.ds(0, peers - 1)]
+                pltpu.make_async_copy(part, part, sem).wait()
+
+        @pl.when(jnp.logical_not(fewer))
+        def _():
+            pltpu.make_async_copy(ref, ref, sem).wait()
+
+    def meet():
+        pl.semaphore_wait(barrier, jnp.where(is_early, n - 1, n))
+        for k in range(peers):
+
+            @pl.when(jnp.logical_not(is_early & (push_k == k)))
+            def _():
+                send_q(k).start()
+
+    meet_at = jnp.where(me == 0, full, jnp.clip((mirror - 1) // 2 * 2 - 1, 0, full))
+
     for k in range(peers):
-        send_q(k).start()
+        slot_s[k] = jnp.maximum(found[k], 0)
+    push_slot = slot_s[push_k]
 
     def scan_next(i, cur):
         j = slots - 1 - i
@@ -182,26 +225,24 @@
     row_id = lax.broadcasted_iota(jnp.int32, (rows, 2 * steps), 0)
     col_id = lax.broadcasted_iota(jnp.int32, (rows, 2 * steps), 1)
     causal[...] = jnp.where((col_id < steps) & (row_id >= col_id * heads), 0.0, -jnp.inf)
-    copy_pool.wait()
 
     factor = math.log2(math.e) / math.sqrt(HDIM)
     key_id = lax.broadcasted_iota(jnp.int32, (1, window), 1)
 
-    def cached(start):
-        return jnp.concatenate([pool[start + b] for b in range(MAXB)], axis=0)
-
-    def attend(items, owners):
+    def cached(j):
+        return jnp.concatenate([pool[off_s[j] + b] for b in range(MAXB)], axis=0)
+
+    def attend(items, caches, lens):
         added = [x[rows:] for x in items]
         new_keys = [x.astype(jnp.bfloat16) for x in added]
         new_values = [pltpu.roll(x, steps, 0).astype(jnp.bfloat16) for x in added]
         items = [x[:rows].astype(jnp.bfloat16) for x in items]
-        starts = [off_s[j] for j in owners]
         scores, fresh = [], []
-        for x, y, j, start in zip(items, new_keys, owners, starts):
+        for x, y, cache, size in zip(items, new_keys, caches, lens):
             s = lax.dot_general(
-                x, cached(start)[:, :HDIM], NT, preferred_element_type=jnp.float32
+                x, cache()[:, :HDIM], NT, preferred_element_type=jnp.float32
             )
-            scores.append(jnp.where(key_id < len_s[me, j] * BLK, s, -jnp.inf))
+            scores.append(jnp.where(key_id < size * BLK, s, -jnp.inf))
             s = lax.dot_general(x, y, NT, preferred_element_type=jnp.float32)
             fresh.append(s + causal[...])
         tops = [
@@ -211,10 +252,10 @@
         scores = [jnp.exp2((s - m) * factor) for s, m in zip(scores, tops)]
         fresh = [jnp.exp2((f - m) * factor) for f, m in zip(fresh, tops)]
         results = []
-        for y, s, f, start in zip(new_values, scores, fresh, starts):
+        for y, s, f, cache in zip(new_values, scores, fresh, caches):
             total = jnp.sum(s, axis=1, keepdims=True) + jnp.sum(f, axis=1, keepdims=True)
             o = jnp.dot(
-                s.astype(jnp.bfloat16), cached(start)[:, HDIM:],
+                s.astype(jnp.bfloat16), cache()[:, HDIM:],
                 preferred_element_type=jnp.float32,
             )
             o = o + jnp.dot(
@@ -223,40 +264,68 @@
             results.append(o / total)
         return results
 
+    def attend_own(items, owners):
+        return attend(
+            items,
+            [functools.partial(cached, j) for j in owners],
+            [len_s[me, j] for j in owners],
+        )
+
     def put(i, value):
         res[i] = value
 
-    def stay_group(base):
-        def run(indices):
-            owners = [stay_s[base + i] for i in indices]
-            for i, o in zip(indices, attend([item_of(j) for j in owners], owners)):
-                put(base + i, o)
-
-        return run
+    def stay_group(indices):
+        owners = [stay_s[i] for i in indices]
+        for i, o in zip(indices, attend_own([item_of(j) for j in owners], owners)):
+            put(i, o)
 
     def move_group(ks):
         owners = [slot_s[k] for k in ks]
-        for k in ks:
-            send_q(k).wait_recv()
+        sent = [(used_s[k] > 0) & jnp.logical_not(is_late & (push_k == k)) for k in ks]
         items = [
-            jnp.where(used_s[k] > 0, q_got[k].astype(jnp.float32), item_of(j))
-            for k, j in zip(ks, owners)
+            jnp.where(ok, q_got[k].astype(jnp.float32), item_of(j))
+            for k, j, ok in zip(ks, owners, sent)
         ]
-        for k, o in zip(ks, attend(items, owners)):
+        for k, o in zip(ks, attend_own(items, owners)):
             put(stays + k, o)
             r_out[k] = o.astype(jnp.bfloat16)
         for k in ks:
-            send_r(k).start()
-
-    early = stays // 2 // 5 * 5
-    grouped(early, 5, stay_group(0))
-    grouped(peers, 7, move_group)
-    grouped(stays - early, 5, stay_group(early))
+
+            @pl.when(jnp.logical_not(is_late & (push_k == k)))
+            def _():
+                send_r(k).start()
+
+    pl.when(meet_at == 0)(meet)
+    copy_pool.wait()
+    for copy in copy_w:
+        copy.start()
+
+    @pl.when(is_late)
+    def _():
+        push_out[...] = pool[off_s[push_slot] + tp]
+        push.start()
+
+    def stay_step(g, carry):
+        stay_group([g * group + u for u in range(group)])
+
+        pl.when(meet_at == g + 1)(meet)
+        return carry
+
+    lax.fori_loop(0, full, stay_step, 0)
+    if stays > full * group:
+        stay_group(list(range(full * group, stays)))
+
+    def serve():
+        all_but_one(is_late, q_got, q_recv)
+        grouped(peers, 7, move_group)
+
+    if not crowded:
+        serve()
 
     def gather(j, carry):
-        own = res[pos_s[j]]
+        own_rows = res[pos_s[j]]
         fin[pl.ds(pl.multiple_of(j * rows, 8), rows), :] = jnp.where(
-            shift_s[j] > 0, jnp.zeros_like(own), own
+            shift_s[j] > 0, jnp.zeros_like(own_rows), own_rows
         )
         return carry
 
@@ -272,6 +341,9 @@
             jnp.bfloat16
         )
         send_o(c).start()
+
+    if crowded:
+        pl.when(me >= MAIN_FIRST)(serve)
     for c in range(chunks):
         copy_w[chunks + c].wait()
         main[c] = jnp.dot(lhs[...], w_buf[chunks + c], preferred_element_type=jnp.float32)
@@ -287,10 +359,28 @@
             (turns > 0) & (col_id == turns + (t * pad - 1)), 1.0, 0.0
         ).astype(jnp.bfloat16)
 
+    @pl.when(is_early)
+    def _():
+        push.wait_recv()
+        relay.start()
+
+    if crowded:
+        pl.when(me < MAIN_FIRST)(serve)
+
+    @pl.when(is_early)
+    def _():
+        relay.wait_recv()
+        (o,) = attend(
+            [item_of(push_slot)],
+            [lambda: jnp.concatenate([push_got[b] for b in range(MAXB)], axis=0)],
+            [len_s[mirror, push_slot]],
+        )
+        r_got[push_k] = o.astype(jnp.bfloat16)
+
+    all_but_one(is_early, r_got, r_recv)
     for k in range(peers, pad):
         back[k] = jnp.zeros((rows, HDIM), jnp.float32)
     for k in range(peers):
-        send_r(k).wait_recv()
         back[k] = r_got[k].astype(jnp.float32)
     flat_back = back.reshape(pad * rows, HDIM)
     for t in range(steps):
@@ -304,21 +394,29 @@
             jnp.bfloat16
         )
         send_m(c).start()
+    pltpu.make_async_copy(o_got, o_got, o_recv).wait()
     for c in range(chunks):
-        own = jnp.dot(moved, w_buf[chunks + c], preferred_element_type=jnp.float32)
-        send_o(c).wait_recv()
+        own[c] = jnp.dot(moved, w_buf[chunks + c], preferred_element_type=jnp.float32)
+        main[c] = main[c] + o_got[c].astype(jnp.float32)
+    for c in range(chunks):
         send_m(c).wait_recv()
-        own = (own + m_got[c].astype(jnp.float32)).astype(jnp.bfloat16)
-        own = jnp.dot(spread[...], own, preferred_element_type=jnp.float32)
-        own = (own + (main[c] + o_got[c].astype(jnp.float32))).astype(out_ref.dtype)
+        total = (own[c] + m_got[c].astype(jnp.float32)).astype(jnp.bfloat16)
+        total = jnp.dot(spread[...], total, preferred_element_type=jnp.float32)
+        total = (total + main[c]).astype(out_ref.dtype)
         for t in range(steps):
-            out_ref[t, :, c * cols : (c + 1) * cols] = own[t * slots : (t + 1) * slots]
-    for k in range(peers):
-        send_q(k).wait_send()
-        send_r(k).wait_send()
-    for c in range(chunks):
-        send_o(c).wait_send()
-        send_m(c).wait_send()
+            out_ref[t, :, c * cols : (c + 1) * cols] = total[t * slots : (t + 1) * slots]
+    all_but_one(is_early, q_out, q_send)
+    all_but_one(is_late, r_out, r_send)
+    pltpu.make_async_copy(o_out, o_out, x_send.at[0]).wait()
+    pltpu.make_async_copy(m_out, m_out, x_send.at[1]).wait()
+
+    @pl.when(is_late)
+    def _():
+        push.wait_send()
+
+    @pl.when(is_early)
+    def _():
+        relay.wait_send()
 
 
 def body(n, queries, new_kv, cache_pool, lengths, anchor, out_weight):
@@ -332,6 +430,7 @@
     peers = n - 1
     pad = -(-peers // 8) * 8
     blocks = cache_pool.shape[0] // BLK
+    edge = min(EDGE, n // 4)
     bf16, f32, i32 = jnp.bfloat16, jnp.float32, jnp.int32
     dma = pltpu.SemaphoreType.DMA
     anywhere = pl.BlockSpec(memory_space=pltpu.HBM)
@@ -341,7 +440,7 @@
         for x in (queries, new_kv, cache, lengths, anchor, out_weight)
     )
     return pl.pallas_call(
-        functools.partial(kernel, n, cols),
+        functools.partial(kernel, n, edge, cols),
         out_shape=jax.ShapeDtypeStruct((steps, slots, half), bf16),
         in_specs=[anywhere] * 6,
         out_specs=pl.BlockSpec(memory_space=pltpu.VMEM),
@@ -364,15 +463,18 @@
             pltpu.VMEM((chunks, steps * pad, cols), bf16),
             pltpu.VMEM((chunks, steps * pad, cols), bf16),
             pltpu.VMEM((chunks, steps * slots, cols), f32),
+            pltpu.VMEM((chunks, steps * pad, cols), f32),
             pltpu.VMEM((pad, rows, HDIM), f32),
             pltpu.VMEM((steps * pad, width), f32),
             pltpu.VMEM((steps * slots, steps * pad), bf16),
+            pltpu.VMEM((BLK, 2 * HDIM), bf16),
+            pltpu.VMEM((MAXB, BLK, 2 * HDIM), bf16),
         ]
         + [pltpu.SMEM(lengths.shape, i32), pltpu.SMEM(anchor.shape, i32)]
         + [pltpu.SMEM((max(slots, n),), i32)] * 8
         + [dma((5,)), dma((2 * chunks,))]
-        + [dma((peers,))] * 4
-        + [dma((chunks,))] * 4,
+        + [dma(())] * 4
+        + [dma((2,)), dma(()), dma((chunks,)), dma((3,))],
         compiler_params=pltpu.CompilerParams(
             collective_id=0, has_side_effects=True, vmem_limit_bytes=48 * 1024 * 1024
         ),

time: 19 us -> 17.7 us (0.932)
  Pallas kernels: 18 us -> 16.8 us
    pallas_call x1, Pallas kernels: 18 us -> 16.8 us  [body(): pl.pallas_call(functools.partial(kernel, n, edge, cols), out_shape=jax.Sh...]
where the time goes in v1:
time: 17.7 us; the launch traced here: 17.6 us
  Pallas kernels  16.8 us (95%)
  local copies, waits for them, and re-layouts  0.75 us (4%)
    pallas_call x1, Pallas kernels, body(): pl.pallas_call(functools.partial(kernel, n, edge, cols), out_shape=jax.Sh...  16.8 us
    unnamed x1, local copies, waits for them, and re-layouts  0.75 us

profile of v1, /device:TPU:0, one launch (start us, length us, event | category | flops | bytes accessed | tf_op | source)
XLA Modules:
  0.0 17.6 jit_solution(4531922608123089076)
XLA Ops:
  0.0 16.8 %shard_map.64 = bf16[4,32,1536]{2,1,0:T(8,128)(2,1)S(1)} custom-call(bf16[4,32,1536]{2,1,0:T(8,128)(2,1)} %q_hbm.1, bf16[4,32,256]{2,1,0:T(8,128)(2,1)} %kv_hbm.1, bf16[48,128,256]{2,1,0:T(8,128)(2,1)} %bitcast.1, s32[8,32]{1,0:T(8,128)} %len_hbm.1, s32[8,32]{1,0:T(8,128)} %anc_hbm.1, bf16[1536,3072]{1,0:T(8,128)(2,1)} %w_hbm.1), custom_call_target="tpu_custom_call" | custom-call | tf_op jit(solution)/shard_map/pallas_call | solution.py:442
  16.8 0.7 %copy.8 = bf16[4,32,1536]{2,1,0:T(8,128)(2,1)} copy(bf16[4,32,1536]{2,1,0:T(8,128)(2,1)S(1)} %shard_map.64) | data formatting | bytes 786432

commit v2 on v1

--- a/solution.py
+++ b/solution.py
@@ -12,8 +12,6 @@
 BLK = 128
 MAXB = 2
 MESH = pl.DeviceIdType.MESH
-EDGE = 1
-MAIN_FIRST = 2
 NT = (((1,), (1,)), ((), ()))
 
 
@@ -57,7 +55,11 @@
     mirror = n - 1 - me
     is_early = me < edge
     is_late = mirror < edge
-    push_k = 2 * jnp.minimum(me, mirror)
+    push_k = 0
+    band = n // 2
+    upper = lax.div(me, band)
+    place = lax.rem(me, band)
+    deepest = lax.div(lax.rem(me + n - 1, n) + 2, n)
 
     copy_len = pltpu.make_async_copy(len_hbm, len_s, in_sem.at[0])
     copy_anc = pltpu.make_async_copy(anc_hbm, anc_s, in_sem.at[1])
@@ -124,10 +126,14 @@
     for k in range(peers):
         q_out[k] = item_of(jnp.maximum(found[k], 0)).astype(jnp.bfloat16)
 
+    def batch_to(k):
+        across = lax.rem(lax.div(lax.rem(me + n - 1 - k, n), band) + upper, 2)
+        return across * (1 + deepest)
+
     def send_q(k):
         return pltpu.make_async_remote_copy(
             src_ref=q_out.at[k], dst_ref=q_got.at[k], send_sem=q_send,
-            recv_sem=q_recv, device_id=peer(n - 1 - k), device_id_type=MESH,
+            recv_sem=q_recv.at[batch_to(k)], device_id=peer(n - 1 - k), device_id_type=MESH,
         )
 
     def send_r(k):
@@ -171,13 +177,19 @@
         def _():
             pltpu.make_async_copy(ref, ref, sem).wait()
 
-    def meet():
+    def greet():
         pl.semaphore_wait(barrier, jnp.where(is_early, n - 1, n))
+
+    def send_all_q():
         for k in range(peers):
 
             @pl.when(jnp.logical_not(is_early & (push_k == k)))
             def _():
                 send_q(k).start()
+
+    def meet():
+        greet()
+        send_all_q()
 
     meet_at = jnp.where(me == 0, full, jnp.clip((mirror - 1) // 2 * 2 - 1, 0, full))
 
@@ -289,7 +301,8 @@
         for k, o in zip(ks, attend_own(items, owners)):
             put(stays + k, o)
             r_out[k] = o.astype(jnp.bfloat16)
-        for k in ks:
+        for i in range(len(ks)):
+            k = upper * ks[len(ks) - 1 - i] + (1 - upper) * ks[i]
 
             @pl.when(jnp.logical_not(is_late & (push_k == k)))
             def _():
@@ -315,12 +328,60 @@
     if stays > full * group:
         stay_group(list(range(full * group, stays)))
 
-    def serve():
-        all_but_one(is_late, q_got, q_recv)
-        grouped(peers, 7, move_group)
-
-    if not crowded:
-        serve()
+    def arrived(count, batch):
+        if count > 0:
+            got = q_got.at[pl.ds(0, count)]
+            pltpu.make_async_copy(got, got, q_recv.at[batch]).wait()
+
+    def serve_near():
+        arrived(band - 1, 0)
+
+        def rotation(i):
+            other = i + lax.div(i + band - place, band)
+            return lax.rem(other - place - 1 + n, n)
+
+        grouped(band - 1, 7, lambda idx: move_group([rotation(i) for i in idx]))
+
+    def far_rotation(i):
+        owner = upper * (band - 1 - i) + (1 - upper) * (band + i)
+        return lax.rem(owner - me - 1 + n, n)
+
+    def serve_shallow():
+        arrived(band - 1, 1)
+        grouped(band - 1, 7, lambda idx: move_group([far_rotation(i) for i in idx]))
+
+    def serve_deep():
+        pl.when(jnp.logical_not(is_late))(lambda: arrived(1, 2))
+        move_group([far_rotation(band - 1)])
+
+    def serve(step):
+        if crowded and step == 1:
+
+            @pl.when(upper > 0)
+            def _():
+                pl.when(jnp.logical_not(is_late))(serve_deep)
+                serve_near()
+                serve_shallow()
+
+            @pl.when((upper == 0) & jnp.logical_not(is_early))
+            def _():
+                serve_near()
+                serve_shallow()
+
+        elif crowded and step == 2:
+
+            @pl.when(is_early)
+            def _():
+                serve_near()
+                serve_shallow()
+
+            pl.when(upper == 0)(serve_deep)
+        elif not crowded and step == 0:
+            serve_near()
+            serve_shallow()
+            serve_deep()
+
+    serve(0)
 
     def gather(j, carry):
         own_rows = res[pos_s[j]]
@@ -342,8 +403,7 @@
         )
         send_o(c).start()
 
-    if crowded:
-        pl.when(me >= MAIN_FIRST)(serve)
+    serve(1)
     for c in range(chunks):
         copy_w[chunks + c].wait()
         main[c] = jnp.dot(lhs[...], w_buf[chunks + c], preferred_element_type=jnp.float32)
@@ -359,13 +419,12 @@
             (turns > 0) & (col_id == turns + (t * pad - 1)), 1.0, 0.0
         ).astype(jnp.bfloat16)
 
+    serve(2)
+
     @pl.when(is_early)
     def _():
         push.wait_recv()
         relay.start()
-
-    if crowded:
-        pl.when(me < MAIN_FIRST)(serve)
 
     @pl.when(is_early)
     def _():
@@ -430,7 +489,7 @@
     peers = n - 1
     pad = -(-peers // 8) * 8
     blocks = cache_pool.shape[0] // BLK
-    edge = min(EDGE, n // 4)
+    edge = min(1, n // 4)
     bf16, f32, i32 = jnp.bfloat16, jnp.float32, jnp.int32
     dma = pltpu.SemaphoreType.DMA
     anywhere = pl.BlockSpec(memory_space=pltpu.HBM)
@@ -473,7 +532,7 @@
         + [pltpu.SMEM(lengths.shape, i32), pltpu.SMEM(anchor.shape, i32)]
         + [pltpu.SMEM((max(slots, n),), i32)] * 8
         + [dma((5,)), dma((2 * chunks,))]
-        + [dma(())] * 4
+        + [dma(()), dma((3,)), dma(()), dma(())]
         + [dma((2,)), dma(()), dma((chunks,)), dma((3,))],
         compiler_params=pltpu.CompilerParams(
             collective_id=0, has_side_effects=True, vmem_limit_bytes=48 * 1024 * 1024

time: 17.7 us -> 17 us (0.960)
  Pallas kernels: 16.8 us -> 16.1 us
    pallas_call x1, Pallas kernels: 16.8 us -> 16.1 us  [body(): pl.pallas_call(functools.partial(kernel, n, edge, cols), out_shape=jax.Sh...]
where the time goes in v2:
time: 17 us; the launch traced here: 16.8 us
  Pallas kernels  16.1 us (95%)
  local copies, waits for them, and re-layouts  0.75 us (4%)
    pallas_call x1, Pallas kernels, body(): pl.pallas_call(functools.partial(kernel, n, edge, cols), out_shape=jax.Sh...  16.1 us
    unnamed x1, local copies, waits for them, and re-layouts  0.75 us

profile of v2, /device:TPU:0, one launch (start us, length us, event | category | flops | bytes accessed | tf_op | source)
XLA Modules:
  0.0 16.8 jit_solution(14023167881958101949)
XLA Ops:
  0.0 16.1 %shard_map.64 = bf16[4,32,1536]{2,1,0:T(8,128)(2,1)S(1)} custom-call(bf16[4,32,1536]{2,1,0:T(8,128)(2,1)} %q_hbm.1, bf16[4,32,256]{2,1,0:T(8,128)(2,1)} %kv_hbm.1, bf16[48,128,256]{2,1,0:T(8,128)(2,1)} %bitcast.1, s32[8,32]{1,0:T(8,128)} %len_hbm.1, s32[8,32]{1,0:T(8,128)} %anc_hbm.1, bf16[1536,3072]{1,0:T(8,128)(2,1)} %w_hbm.1), custom_call_target="tpu_custom_call" | custom-call | tf_op jit(solution)/shard_map/pallas_call | solution.py:501
  16.1 0.7 %copy.8 = bf16[4,32,1536]{2,1,0:T(8,128)(2,1)} copy(bf16[4,32,1536]{2,1,0:T(8,128)(2,1)S(1)} %shard_map.64) | data formatting | bytes 786432

commit v3 on v2

--- a/solution.py
+++ b/solution.py
@@ -142,18 +142,14 @@
             recv_sem=r_recv, device_id=peer(k + 1), device_id_type=MESH,
         )
 
-    def send_o(c):
-        return pltpu.make_async_remote_copy(
-            src_ref=o_out.at[c], dst_ref=o_got.at[c], send_sem=x_send.at[0],
-            recv_sem=o_recv, device_id={"tp": 1 - tp}, device_id_type=MESH,
-        )
-
-    def send_m(c):
-        return pltpu.make_async_remote_copy(
-            src_ref=m_out.at[c], dst_ref=m_got.at[c], send_sem=x_send.at[1],
-            recv_sem=m_recv.at[c], device_id={"tp": 1 - tp}, device_id_type=MESH,
-        )
-
+    send_o = pltpu.make_async_remote_copy(
+        src_ref=o_out, dst_ref=o_got, send_sem=x_send.at[0],
+        recv_sem=o_recv, device_id={"tp": 1 - tp}, device_id_type=MESH,
+    )
+    send_m = pltpu.make_async_remote_copy(
+        src_ref=m_out, dst_ref=m_got, send_sem=x_send.at[1],
+        recv_sem=m_recv, device_id={"tp": 1 - tp}, device_id_type=MESH,
+    )
     push = pltpu.make_async_remote_copy(
         src_ref=push_out, dst_ref=push_got.at[tp], send_sem=p_sem.at[0],
         recv_sem=p_sem.at[1], device_id={"inst": mirror}, device_id_type=MESH,
@@ -398,14 +394,16 @@
             ].astype(jnp.bfloat16)
     for c in range(chunks):
         copy_w[c].wait()
+    for c in range(chunks):
         o_out[c] = jnp.dot(lhs[...], w_buf[c], preferred_element_type=jnp.float32).astype(
             jnp.bfloat16
         )
-        send_o(c).start()
+    send_o.start()
 
     serve(1)
     for c in range(chunks):
         copy_w[chunks + c].wait()
+    for c in range(chunks):
         main[c] = jnp.dot(lhs[...], w_buf[chunks + c], preferred_element_type=jnp.float32)
 
     pad = back.shape[0]
@@ -452,13 +450,13 @@
         m_out[c] = jnp.dot(moved, w_buf[c], preferred_element_type=jnp.float32).astype(
             jnp.bfloat16
         )
-        send_m(c).start()
-    pltpu.make_async_copy(o_got, o_got, o_recv).wait()
+    send_m.start()
+    send_o.wait_recv()
     for c in range(chunks):
         own[c] = jnp.dot(moved, w_buf[chunks + c], preferred_element_type=jnp.float32)
         main[c] = main[c] + o_got[c].astype(jnp.float32)
-    for c in range(chunks):
-        send_m(c).wait_recv()
+    send_m.wait_recv()
+    for c in range(chunks):
         total = (own[c] + m_got[c].astype(jnp.float32)).astype(jnp.bfloat16)
         total = jnp.dot(spread[...], total, preferred_element_type=jnp.float32)
         total = (total + main[c]).astype(out_ref.dtype)
@@ -466,8 +464,8 @@
             out_ref[t, :, c * cols : (c + 1) * cols] = total[t * slots : (t + 1) * slots]
     all_but_one(is_early, q_out, q_send)
     all_but_one(is_late, r_out, r_send)
-    pltpu.make_async_copy(o_out, o_out, x_send.at[0]).wait()
-    pltpu.make_async_copy(m_out, m_out, x_send.at[1]).wait()
+    send_o.wait_send()
+    send_m.wait_send()
 
     @pl.when(is_late)
     def _():
@@ -533,7 +531,7 @@
         + [pltpu.SMEM((max(slots, n),), i32)] * 8
         + [dma((5,)), dma((2 * chunks,))]
         + [dma(()), dma((3,)), dma(()), dma(())]
-        + [dma((2,)), dma(()), dma((chunks,)), dma((3,))],
+        + [dma((2,)), dma(()), dma(()), dma((3,))],
         compiler_params=pltpu.CompilerParams(
             collective_id=0, has_side_effects=True, vmem_limit_bytes=48 * 1024 * 1024
         ),

time: 17 us -> 16.7 us (0.982)
  the two profiles are of different devices: /device:TPU:0 before, /device:TPU:7 now
where the time goes in v3:
time: 16.7 us; the launch traced here: 16.6 us
  Pallas kernels  15.8 us (95%)
  local copies, waits for them, and re-layouts  0.75 us (4%)
    pallas_call x1, Pallas kernels, body(): pl.pallas_call(functools.partial(kernel, n, edge, cols), out_shape=jax.Sh...  15.8 us
    unnamed x1, local copies, waits for them, and re-layouts  0.75 us

profile of v3, /device:TPU:7, one launch (start us, length us, event | category | flops | bytes accessed | tf_op | source)
XLA Modules:
  0.0 16.6 jit_solution(3348239762397061117)
XLA Ops:
  0.0 15.8 %shard_map.64 = bf16[4,32,1536]{2,1,0:T(8,128)(2,1)S(1)} custom-call(bf16[4,32,1536]{2,1,0:T(8,128)(2,1)} %q_hbm.1, bf16[4,32,256]{2,1,0:T(8,128)(2,1)} %kv_hbm.1, bf16[48,128,256]{2,1,0:T(8,128)(2,1)} %bitcast.1, s32[8,32]{1,0:T(8,128)} %len_hbm.1, s32[8,32]{1,0:T(8,128)} %anc_hbm.1, bf16[1536,3072]{1,0:T(8,128)(2,1)} %w_hbm.1), custom_call_target="tpu_custom_call" | custom-call | tf_op jit(solution)/shard_map/pallas_call | solution.py:499
  15.8 0.7 %copy.8 = bf16[4,32,1536]{2,1,0:T(8,128)(2,1)} copy(bf16[4,32,1536]{2,1,0:T(8,128)(2,1)S(1)} %shard_map.64) | data formatting | bytes 786432

commit v4 on v3

--- a/solution.py
+++ b/solution.py
@@ -356,8 +356,8 @@
             @pl.when(upper > 0)
             def _():
                 pl.when(jnp.logical_not(is_late))(serve_deep)
+                serve_shallow()
                 serve_near()
-                serve_shallow()
 
             @pl.when((upper == 0) & jnp.logical_not(is_early))
             def _():

time: 16.7 us -> 16.3 us (0.976)
  the two profiles are of different devices: /device:TPU:7 before, /device:TPU:0 now
where the time goes in v4:
time: 16.3 us; the launch traced here: 16.2 us
  Pallas kernels  15.4 us (94%)
  local copies, waits for them, and re-layouts  0.75 us (5%)
    pallas_call x1, Pallas kernels, body(): pl.pallas_call(functools.partial(kernel, n, edge, cols), out_shape=jax.Sh...  15.4 us
    unnamed x1, local copies, waits for them, and re-layouts  0.75 us

profile of v4, /device:TPU:0, one launch (start us, length us, event | category | flops | bytes accessed | tf_op | source)
XLA Modules:
  0.0 16.2 jit_solution(5500961535126279337)
XLA Ops:
  0.0 15.4 %shard_map.64 = bf16[4,32,1536]{2,1,0:T(8,128)(2,1)S(1)} custom-call(bf16[4,32,1536]{2,1,0:T(8,128)(2,1)} %q_hbm.1, bf16[4,32,256]{2,1,0:T(8,128)(2,1)} %kv_hbm.1, bf16[48,128,256]{2,1,0:T(8,128)(2,1)} %bitcast.1, s32[8,32]{1,0:T(8,128)} %len_hbm.1, s32[8,32]{1,0:T(8,128)} %anc_hbm.1, bf16[1536,3072]{1,0:T(8,128)(2,1)} %w_hbm.1), custom_call_target="tpu_custom_call" | custom-call | tf_op jit(solution)/shard_map/pallas_call | solution.py:499
  15.4 0.7 %copy.8 = bf16[4,32,1536]{2,1,0:T(8,128)(2,1)} copy(bf16[4,32,1536]{2,1,0:T(8,128)(2,1)S(1)} %shard_map.64) | data formatting | bytes 786432

commit v5 on v4

--- a/solution.py
+++ b/solution.py
@@ -61,6 +61,18 @@
     place = lax.rem(me, band)
     deepest = lax.div(lax.rem(me + n - 1, n) + 2, n)
 
+    def peer(k):
+        return {"inst": lax.rem(me + k, n)}
+
+    barrier = pltpu.get_barrier_semaphore()
+    for k in range(peers):
+
+        @pl.when(jnp.logical_not(is_late & (push_k == k)))
+        def _():
+            pl.semaphore_signal(barrier, inc=1, device_id=peer(k + 1), device_id_type=MESH)
+
+    pl.semaphore_signal(barrier, inc=1, device_id={"tp": 1 - tp}, device_id_type=MESH)
+
     copy_len = pltpu.make_async_copy(len_hbm, len_s, in_sem.at[0])
     copy_anc = pltpu.make_async_copy(anc_hbm, anc_s, in_sem.at[1])
     copy_q = pltpu.make_async_copy(q_hbm, q_in, in_sem.at[2])
@@ -79,18 +91,6 @@
             pltpu.make_async_copy(w_hbm.at[:, pl.ds(column, cols)], w_buf.at[c], w_sem.at[c])
         )
 
-    def peer(k):
-        return {"inst": lax.rem(me + k, n)}
-
-    barrier = pltpu.get_barrier_semaphore()
-    for k in range(peers):
-
-        @pl.when(jnp.logical_not(is_late & (push_k == k)))
-        def _():
-            pl.semaphore_signal(barrier, inc=1, device_id=peer(k + 1), device_id_type=MESH)
-
-    pl.semaphore_signal(barrier, inc=1, device_id={"tp": 1 - tp}, device_id_type=MESH)
-
     def scan_slot(j, carry):
         off, found = carry
         turn = me - anc_s[me, j]
@@ -187,7 +187,7 @@
         greet()
         send_all_q()
 
-    meet_at = jnp.where(me == 0, full, jnp.clip((mirror - 1) // 2 * 2 - 1, 0, full))
+    meet_at = jnp.where(me == 0, full, jnp.clip((mirror - 1) // 2 * 2 - 2, 0, full))
 
     for k in range(peers):
         slot_s[k] = jnp.maximum(found[k], 0)

time: 16.3 us -> 16.3 us (level)
  no operation moved by 1% of the time
where the time goes in v5:
time: 16.3 us; the launch traced here: 16.2 us
  Pallas kernels  15.4 us (94%)
  local copies, waits for them, and re-layouts  0.75 us (5%)
    pallas_call x1, Pallas kernels, body(): pl.pallas_call(functools.partial(kernel, n, edge, cols), out_shape=jax.Sh...  15.4 us
    unnamed x1, local copies, waits for them, and re-layouts  0.75 us

profile of v5, /device:TPU:0, one launch (start us, length us, event | category | flops | bytes accessed | tf_op | source)
XLA Modules:
  0.0 16.2 jit_solution(6692525840462730173)
XLA Ops:
  0.0 15.4 %shard_map.64 = bf16[4,32,1536]{2,1,0:T(8,128)(2,1)S(1)} custom-call(bf16[4,32,1536]{2,1,0:T(8,128)(2,1)} %q_hbm.1, bf16[4,32,256]{2,1,0:T(8,128)(2,1)} %kv_hbm.1, bf16[48,128,256]{2,1,0:T(8,128)(2,1)} %bitcast.1, s32[8,32]{1,0:T(8,128)} %len_hbm.1, s32[8,32]{1,0:T(8,128)} %anc_hbm.1, bf16[1536,3072]{1,0:T(8,128)(2,1)} %w_hbm.1), custom_call_target="tpu_custom_call" | custom-call | tf_op jit(solution)/shard_map/pallas_call | solution.py:499
  15.4 0.7 %copy.8 = bf16[4,32,1536]{2,1,0:T(8,128)(2,1)} copy(bf16[4,32,1536]{2,1,0:T(8,128)(2,1)S(1)} %shard_map.64) | data formatting | bytes 786432

commit v6 on v5

--- a/solution.py
+++ b/solution.py
@@ -88,7 +88,7 @@
         side = (1 - tp) if c < chunks else tp
         column = pl.multiple_of(side * half + (c % chunks) * cols, cols)
         copy_w.append(
-            pltpu.make_async_copy(w_hbm.at[:, pl.ds(column, cols)], w_buf.at[c], w_sem.at[c])
+            pltpu.make_async_copy(w_hbm.at[:, pl.ds(column, cols)], w_buf.at[c], w_sem.at[c // chunks])
         )
 
     def scan_slot(j, carry):
@@ -392,8 +392,8 @@
             lhs[t * slots : (t + 1) * slots, h * HDIM : (h + 1) * HDIM] = fin[
                 pl.ds(t * heads + h, slots, stride=rows), :
             ].astype(jnp.bfloat16)
-    for c in range(chunks):
-        copy_w[c].wait()
+    weights = w_buf.at[pl.ds(0, chunks)]
+    pltpu.make_async_copy(weights, weights, w_sem.at[0]).wait()
     for c in range(chunks):
         o_out[c] = jnp.dot(lhs[...], w_buf[c], preferred_element_type=jnp.float32).astype(
             jnp.bfloat16
@@ -401,8 +401,8 @@
     send_o.start()
 
     serve(1)
-    for c in range(chunks):
-        copy_w[chunks + c].wait()
+    weights = w_buf.at[pl.ds(chunks, chunks)]
+    pltpu.make_async_copy(weights, weights, w_sem.at[1]).wait()
     for c in range(chunks):
         main[c] = jnp.dot(lhs[...], w_buf[chunks + c], preferred_element_type=jnp.float32)
 
@@ -529,7 +529,7 @@
         ]
         + [pltpu.SMEM(lengths.shape, i32), pltpu.SMEM(anchor.shape, i32)]
         + [pltpu.SMEM((max(slots, n),), i32)] * 8
-        + [dma((5,)), dma((2 * chunks,))]
+        + [dma((5,)), dma((2,))]
         + [dma(()), dma((3,)), dma(()), dma(())]
         + [dma((2,)), dma(()), dma(()), dma((3,))],
         compiler_params=pltpu.CompilerParams(

time: 16.3 us -> 16.3 us (level)
  no operation moved by 1% of the time
where the time goes in v6:
time: 16.3 us; the launch traced here: 16.1 us
  Pallas kernels  15.4 us (94%)
  local copies, waits for them, and re-layouts  0.75 us (5%)
    pallas_call x1, Pallas kernels, body(): pl.pallas_call(functools.partial(kernel, n, edge, cols), out_shape=jax.Sh...  15.4 us
    unnamed x1, local copies, waits for them, and re-layouts  0.75 us

profile of v6, /device:TPU:0, one launch (start us, length us, event | category | flops | bytes accessed | tf_op | source)
XLA Modules:
  0.0 16.1 jit_solution(4880943852676493982)
XLA Ops:
  0.0 15.4 %shard_map.64 = bf16[4,32,1536]{2,1,0:T(8,128)(2,1)S(1)} custom-call(bf16[4,32,1536]{2,1,0:T(8,128)(2,1)} %q_hbm.1, bf16[4,32,256]{2,1,0:T(8,128)(2,1)} %kv_hbm.1, bf16[48,128,256]{2,1,0:T(8,128)(2,1)} %bitcast.1, s32[8,32]{1,0:T(8,128)} %len_hbm.1, s32[8,32]{1,0:T(8,128)} %anc_hbm.1, bf16[1536,3072]{1,0:T(8,128)(2,1)} %w_hbm.1), custom_call_target="tpu_custom_call" | custom-call | tf_op jit(solution)/shard_map/pallas_call | solution.py:499
  15.4 0.7 %copy.8 = bf16[4,32,1536]{2,1,0:T(8,128)(2,1)} copy(bf16[4,32,1536]{2,1,0:T(8,128)(2,1)S(1)} %shard_map.64) | data formatting | bytes 786432
